TPU v7x, 256 devices: a whole 4x4x8 slice. The times are simulated.
256 devices in a mesh: row: 8 (over y, z_hi), col: 32 (over z_lo, x, core).
Axes of the slice: x: 4, y: 4, z: 8 (z_hi: 2, z_lo: 4; z = z_hi * 4 + z_lo), core: 2. Of those that a mesh axis runs over, the one named last changes fastest.
Arguments:
- embedding: bfloat16 [98304, 256], P(('col', 'row')), may hold values from -6 to 6
- weight: bfloat16 [256, 256], replicated, may hold values from -0.375 to 0.375
- grad_out: bfloat16 [98304, 256], P(('row', 'col')), may hold values from -6 to 6
- in_degree: int32 [98304], P(('row', 'col')), may hold values from 4 to 64
- out_degree: int32 [98304], P(('col', 'row')), may hold values from 4 to 64
- tile_edges: bfloat16 [8, 32, 192, 128, 128], P('row', 'col'), may hold values from 0 to 2, as said below
- tile_coords: int32 [8, 32, 192, 2], P('row', 'col'), may hold values from 0 to 95, as said below
- tile_count: int32 [8, 32], P('row', 'col'), may hold values from 48 to 192, as said below
Outputs:
- hidden: bfloat16 [98304, 256], P(('row', 'col'))
- grad_embedding: float32 [98304, 256], P(('col', 'row'))
- grad_weight: float32 [256, 256], replicated
Inputs may be any that keep to these rules, and one draw needn't show every extreme that they name: `tile_coords`: slots of one block name distinct tiles; entry 0 is a tile row below 96, entry 1 a tile column below 24. The live slots of a block are its first tile_count slots; some block has all 192 slots live. `tile_edges`: each entry is zero or a positive edge weight.
All inputs are finite; a program needn't handle non-finite values.
Results may differ from a plain program's by a relative error of at most 0.033.
Values may be sent and summed in bfloat16 or wider, within the bound.
No kernel may reach another device: no remote copies, remote signals or barrier semaphores. Data moves between devices by JAX's collectives and lax.ppermute only.
A program may use at most 128 MiB of HBM per device.

v0:
```python
import math
import jax
import jax.numpy as jnp
from jax import lax
from jax.sharding import PartitionSpec as P

decay_rate = 0.01


def tile_products(tile_set, source_ids, target_ids, alive, lookup, out_count, flipped):
    slots = tile_set.shape[0]
    block_count = max(1, slots // 64)
    per_block = slots // block_count

    def advance(running, number):
        first_slot = number * per_block
        block_tiles = lax.dynamic_slice_in_dim(tile_set, first_slot, per_block, 0)
        chosen = lax.dynamic_slice_in_dim(source_ids, first_slot, per_block, 0)
        picked = jnp.take(lookup, chosen, axis=0)
        if flipped:
            products = jnp.einsum(
                "tij,tif->tjf", block_tiles, picked, preferred_element_type=jnp.float32
            )
        else:
            products = jnp.einsum(
                "tij,tjf->tif", block_tiles, picked, preferred_element_type=jnp.float32
            )
        targets = lax.dynamic_slice_in_dim(target_ids, first_slot, per_block, 0)
        weights_alive = lax.dynamic_slice_in_dim(alive, first_slot, per_block, 0)
        products = products * weights_alive[:, None, None]
        running = running + jax.ops.segment_sum(products, targets, num_segments=out_count)
        return (running, None)

    initial = jnp.zeros((out_count, lookup.shape[1], lookup.shape[2]), jnp.float32)
    result, _ = lax.scan(advance, initial, jnp.arange(block_count))
    return result


def per_device(
    embedding, weight, grad_out, in_degree, out_degree, tile_edges, tile_coords, tile_count
):
    tile_set = tile_edges[0, 0]
    coords = tile_coords[0, 0]
    live_count = tile_count[0, 0]
    n_row = lax.axis_size("row")
    n_col = lax.axis_size("col")
    own_rows, width = embedding.shape
    edge_size = tile_set.shape[1]
    block_rows = own_rows * n_col
    block_cols = own_rows * n_row
    tile_rows = block_rows // edge_size
    tile_cols = block_cols // edge_size
    total_nodes = own_rows * n_row * n_col
    alive = (jnp.arange(tile_set.shape[0]) < live_count).astype(jnp.float32)
    scale_out = lax.rsqrt(out_degree.astype(jnp.float32))
    scaled = (scale_out[:, None] * embedding.astype(jnp.float32)).astype(jnp.bfloat16)
    source_block = lax.all_gather(scaled, "row", axis=0, tiled=True)
    forward_terms = tile_products(
        tile_set,
        coords[:, 1],
        coords[:, 0],
        alive,
        source_block.reshape(tile_cols, edge_size, width),
        tile_rows,
        False,
    )
    forward_terms = forward_terms.reshape(block_rows, width)
    summed = lax.psum_scatter(
        forward_terms.astype(jnp.bfloat16), "col", scatter_dimension=0, tiled=True
    ).astype(jnp.float32)
    scale_in = lax.rsqrt(in_degree.astype(jnp.float32))
    aggregate = (scale_in[:, None] * summed).astype(jnp.bfloat16)
    preact = jnp.dot(aggregate, weight, preferred_element_type=jnp.float32)
    gates = jax.nn.sigmoid(preact)
    hidden = (preact * gates).astype(jnp.bfloat16)
    delta_rows = (grad_out.astype(jnp.float32) * gates * (1.0 + preact * (1.0 - gates))).astype(
        jnp.bfloat16
    )
    local_weight = lax.dot_general(
        aggregate, delta_rows, (((0,), (0,)), ((), ())), preferred_element_type=jnp.float32
    )
    grad_weight = lax.psum(local_weight, ("row", "col")) / math.sqrt(total_nodes)
    projected = lax.dot_general(
        delta_rows, weight, (((1,), (1,)), ((), ())), preferred_element_type=jnp.float32
    )
    upstream = (scale_in[:, None] * projected).astype(jnp.bfloat16)
    upstream_block = lax.all_gather(upstream, "col", axis=0, tiled=True)
    backward_terms = tile_products(
        tile_set,
        coords[:, 0],
        coords[:, 1],
        alive,
        upstream_block.reshape(tile_rows, edge_size, width),
        tile_cols,
        True,
    )
    backward_terms = backward_terms.reshape(block_cols, width)
    source_total = lax.psum_scatter(
        backward_terms.astype(jnp.bfloat16), "row", scatter_dimension=0, tiled=True
    ).astype(jnp.float32)
    decay = decay_rate * jnp.sqrt(out_degree.astype(jnp.float32))
    grad_embedding = scale_out[:, None] * source_total + decay[:, None] * embedding.astype(
        jnp.float32
    )
    return (hidden, grad_embedding, grad_weight)


def solution(mesh):
    in_specs = (
        P(("col", "row"), None),
        P(),
        P(("row", "col"), None),
        P(("row", "col")),
        P(("col", "row")),
        P("row", "col", None, None, None),
        P("row", "col", None, None),
        P("row", "col"),
    )
    out_specs = (P(("row", "col"), None), P(("col", "row"), None), P())
    return jax.shard_map(
        per_device, mesh=mesh, in_specs=in_specs, out_specs=out_specs, check_vma=False
    )
```

profile of v0, /device:TPU:2, one launch (start us, length us, event | category | flops | bytes accessed | tf_op | source)
XLA Modules:
  0.0 763.7 jit_solution(9937921684894183327)
XLA Ops:
  12.3 71.1 %all-gather.3.cloned.1.call-done = bf16[3072,256]{1,0:T(8,128)(2,1)} async-done(((bf16[384,256]{1,0:T(8,128)(2,1)}), bf16[3072,256]{1,0:T(8,128)(2,1)}) %all-gather.3.cloned.1.call-update) | async-done | bytes 1572880 | tf_op jit(solution)/shard_map/all_gather | solution.py:57
  83.4 6.1 broadcast.23
  89.5 94.0 %while.20 = (s32[]{:T(128)}, f32[96,128,256]{2,1,0:T(8,128)}, s32[3]{0:T(128)S(1)}, s32[192]{0:T(256)S(1)}, bf16[192,128,128]{2,1,0:T(8,128)(2,1)}, /*index=5*/s...) while((s32[]{:T(128)}, f32[96,128,256]{2,1,0:T(8,128)}, ...), condition=%wide.region_2.3_spmd, body=%wide.region_0.2_spmd.sunk | while | flops 543163776 | bytes 48241472 | solution.py:35
  93.7 7.4 broadcast_multiply_fusion.5
  101.1 19.7 %scatter_fusion = f32[96,128,256]{2,1,0:T(8,128)} fusion(f32[96,128,256]{2,1,0:T(8,128)} %get-tuple-element.258, s32[64]{0:T(128)S(1)} %dynamic_slice.49, f32[64,128,256]{2,1,0:T(8,128)} %broadcast_multiply_fusion.5), kind=kCustom, calls=%fused_computation.2.clone.1 | custom fusion | flops 2097152 | bytes 25166080 | tf_op jit(solution)/shard_map/while/body/eval_jaxpr/scatter-add | solution.py:31
  125.0 7.4 broadcast_multiply_fusion.5
  132.4 19.8 %scatter_fusion = f32[96,128,256]{2,1,0:T(8,128)} fusion(f32[96,128,256]{2,1,0:T(8,128)} %get-tuple-element.258, s32[64]{0:T(128)S(1)} %dynamic_slice.49, f32[64,128,256]{2,1,0:T(8,128)} %broadcast_multiply_fusion.5), kind=kCustom, calls=%fused_computation.2.clone.1 | custom fusion | flops 2097152 | bytes 25166080 | tf_op jit(solution)/shard_map/while/body/eval_jaxpr/scatter-add | solution.py:31
  156.4 7.4 broadcast_multiply_fusion.5
  163.8 19.6 %scatter_fusion = f32[96,128,256]{2,1,0:T(8,128)} fusion(f32[96,128,256]{2,1,0:T(8,128)} %get-tuple-element.258, s32[64]{0:T(128)S(1)} %dynamic_slice.49, f32[64,128,256]{2,1,0:T(8,128)} %broadcast_multiply_fusion.5), kind=kCustom, calls=%fused_computation.2.clone.1 | custom fusion | flops 2097152 | bytes 25166080 | tf_op jit(solution)/shard_map/while/body/eval_jaxpr/scatter-add | solution.py:31
  183.4 8.1 %convert_element_type.55 = bf16[96,128,256]{2,1,0:T(8,128)(2,1)} convert(f32[96,128,256]{2,1,0:T(8,128)} %get-tuple-element.87) | non-fusion elementwise | flops 3145728 | bytes 18874368 | tf_op jit(solution)/shard_map/convert_element_type | solution.py:69
  192.2 143.5 %reduce-scatter.3.cloned.1.call-done = bf16[384,256]{1,0:T(8,128)(2,1)} async-done(((bf16[12288,256]{1,0:T(8,128)(2,1)}), bf16[384,256]{1,0:T(8,128)(2,1)}) %reduce-scatter.3.cloned.1.call-update) | async-done | bytes 196624 | tf_op jit(solution)/shard_map/reduce_scatter | solution.py:68
  338.8 8.7 %copy.11 = bf16[1,1,192,128,128]{3,4,2,1,0:T(8,128)(2,1)} copy(bf16[1,1,192,128,128]{4,3,2,1,0:T(8,128)(2,1)} %bitcast.24) | data formatting | bytes 12582912 | tf_op args[5]
  348.6 58.1 %all-gather.5.cloned.1.call-done = bf16[12288,256]{1,0:T(8,128)(2,1)} async-done(((bf16[384,256]{1,0:T(8,128)(2,1)}), bf16[12288,256]{1,0:T(8,128)(2,1)}) %all-gather.5.cloned.1.call-update) | async-done | bytes 6291472 | tf_op jit(solution)/shard_map/all_gather | solution.py:87
  407.0 80.9 %while.21 = (s32[]{:T(128)}, f32[24,128,256]{2,1,0:T(8,128)S(1)}, s32[3]{0:T(128)S(1)}, s32[192]{0:T(256)S(1)}, bf16[192,128,128]{1,2,0:T(8,128)(2,1)}, /*index=...) while((s32[]{:T(128)}, f32[24,128,256]{2,1,0:T(8,128)S(1)}, ...), condition=%wide.region_6.7_spmd, body=%wide.region_4.6_spmd.sunk | while | flops 543163776 | bytes 48241472 | solution.py:35
  414.0 7.4 broadcast_multiply_fusion.6
  421.5 12.5 %scatter_fusion.1 = f32[24,128,256]{2,1,0:T(8,128)S(1)} fusion(f32[24,128,256]{2,1,0:T(8,128)S(1)} %get-tuple-element.294, s32[64]{0:T(128)S(1)} %dynamic_slice.53, f32[64,128,256]{2,1,0:T(8,128)} %broadcast_multiply_fusion.6), kind=kCustom, calls=%fused_computation.3.clone.1 | custom fusion | flops 2097152 | bytes 25166080 | tf_op jit(solution)/shard_map/while/body/eval_jaxpr/scatter-add | solution.py:31
  435.3 5.6 gather_fusion.1
  441.0 7.4 broadcast_multiply_fusion.6
  448.4 12.5 %scatter_fusion.1 = f32[24,128,256]{2,1,0:T(8,128)S(1)} fusion(f32[24,128,256]{2,1,0:T(8,128)S(1)} %get-tuple-element.294, s32[64]{0:T(128)S(1)} %dynamic_slice.53, f32[64,128,256]{2,1,0:T(8,128)} %broadcast_multiply_fusion.6), kind=kCustom, calls=%fused_computation.3.clone.1 | custom fusion | flops 2097152 | bytes 25166080 | tf_op jit(solution)/shard_map/while/body/eval_jaxpr/scatter-add | solution.py:31
  462.3 5.6 gather_fusion.1
  468.0 7.4 broadcast_multiply_fusion.6
  475.4 12.5 %scatter_fusion.1 = f32[24,128,256]{2,1,0:T(8,128)S(1)} fusion(f32[24,128,256]{2,1,0:T(8,128)S(1)} %get-tuple-element.294, s32[64]{0:T(128)S(1)} %dynamic_slice.53, f32[64,128,256]{2,1,0:T(8,128)} %broadcast_multiply_fusion.6), kind=kCustom, calls=%fused_computation.3.clone.1 | custom fusion | flops 2097152 | bytes 25166080 | tf_op jit(solution)/shard_map/while/body/eval_jaxpr/scatter-add | solution.py:31
  489.4 172.9 %all-reduce.2.cloned.1.call-done = f32[256,256]{1,0:T(8,128)} async-done(((f32[256,256]{1,0:T(8,128)}), f32[256,256]{1,0:T(8,128)}) %all-reduce.2.cloned.1.call-update) | async-done | bytes 262160 | tf_op jit(solution)/shard_map/psum | solution.py:82
  664.0 91.3 %reduce-scatter.5.cloned.1.call-done = bf16[384,256]{1,0:T(8,128)(2,1)} async-done(((bf16[3072,256]{1,0:T(8,128)(2,1)}), bf16[384,256]{1,0:T(8,128)(2,1)}) %reduce-scatter.5.cloned.1.call-update) | async-done | bytes 196624 | tf_op jit(solution)/shard_map/reduce_scatter | solution.py:98
  (78 shorter events, 33.3 us)
Async XLA Ops:
  7.2 328.6 %copy-start = (bf16[256,256]{1,0:T(8,128)(2,1)S(1)}, bf16[256,256]{1,0:T(8,128)(2,1)}, u32[]{:S(2)}) copy-start(bf16[256,256]{1,0:T(8,128)(2,1)} %param.13) | copy-start | bytes 393220
  7.2 76.2 %all-gather.3.cloned.1.call-start = ((), (), s32[]{:S(2)}) async-start(), calls=%async_computation.2 | async-start | bytes 1769472 | tf_op jit(solution)/shard_map/all_gather | solution.py:57
  8.5 0.5 copy-start.5
  10.8 324.9 %reduce-scatter.3.cloned.1.call-start = ((), (), s32[]{:S(2)}) async-start(), calls=%async_computation.3 | async-start | bytes 6488064 | tf_op jit(solution)/shard_map/reduce_scatter | solution.py:68
  83.4 6.1 copy-start.2
  191.6 0.7 copy-start.8
  191.6 144.2 %copy-start.9 = (bf16[384,256]{1,0:T(8,128)(2,1)S(1)}, bf16[384,256]{1,0:T(8,128)(2,1)}, u32[]{:S(2)}) copy-start(bf16[384,256]{1,0:T(8,128)(2,1)} %param.14) | copy-start | bytes 589828
  191.6 215.1 %all-gather.5.cloned.1.call-start = ((), (), s32[]{:S(2)}) async-start(), calls=%async_computation.4 | async-start | bytes 6488064 | tf_op jit(solution)/shard_map/all_gather | solution.py:87
  338.7 8.8 %copy-start.4 = (bf16[384,256]{1,0:T(8,128)(2,1)S(1)}, bf16[384,256]{1,0:T(8,128)(2,1)}, u32[]{:S(2)}) copy-start(bf16[384,256]{1,0:T(8,128)(2,1)} %reduce-scatter.3.cloned.1.call-done) | copy-start | bytes 589828
  338.7 323.6 %all-reduce.2.cloned.1.call-start = ((), (), s32[]{:S(2)}) async-start(), calls=%async_computation.6 | async-start | bytes 524288 | tf_op jit(solution)/shard_map/psum | solution.py:82
  348.6 406.7 %reduce-scatter.5.cloned.1.call-start = ((), (), s32[]{:S(2)}) async-start(), calls=%async_computation.5 | async-start | bytes 1769472 | tf_op jit(solution)/shard_map/reduce_scatter | solution.py:98
  487.9 267.4 %copy-start.3 = (bf16[384,256]{1,0:T(8,128)(2,1)S(1)}, bf16[384,256]{1,0:T(8,128)(2,1)}, u32[]{:S(2)}) copy-start(bf16[384,256]{1,0:T(8,128)(2,1)} %param.12) | copy-start | bytes 589828
  487.9 267.4 %copy-start.6 = (f32[384]{0:T(512)S(1)}, f32[384]{0:T(512)}, u32[]{:S(2)}) copy-start(f32[384]{0:T(512)} %copy-done.5) | copy-start | bytes 4612
  487.9 267.3 %copy-start.7 = (f32[384]{0:T(512)S(1)}, f32[384]{0:T(512)}, u32[]{:S(2)}) copy-start(f32[384]{0:T(512)} %get-tuple-element.135) | copy-start | bytes 4612
  487.9 269.2 %copy-start.1 = (bf16[256,256]{1,0:T(8,128)(2,1)S(1)}, bf16[256,256]{1,0:T(8,128)(2,1)}, u32[]{:S(2)}) copy-start(bf16[256,256]{1,0:T(8,128)(2,1)} %param.13) | copy-start | bytes 393220
Sparse Core Ops, SparseCore 0:
  11.2 72.1 all-gather.2
  191.7 143.9 reduce-scatter.2
  338.8 67.8 all-gather.4
  412.6 249.7 all-reduce.1
  666.2 89.0 reduce-scatter.4
where the time goes:
time: 765 us; the launch traced here: 764 us
  waiting for transfers between devices  537 us (70%)
  other arithmetic  113 us (15%)
  matrix products  48.2 us (6%)
  local copies, waits for them, and re-layouts  46.6 us (6%)
  between operations  14.5 us (2%)
    psum x1, waiting for transfers between devices, per_device(): lax.psum(local_weight, ('row', 'col')) / math.sqrt(total_nodes)  173 us
    reduce_scatter x1, waiting for transfers between devices, per_device(): lax.psum_scatter(forward_terms.astype(jnp.bfloat16), 'col', scatter_dimen...  143 us
    scatter-add x6, other arithmetic, advance(): jax.ops.segment_sum(products, targets, num_segments=out_count)  96.5 us
    reduce_scatter x1, waiting for transfers between devices, per_device(): lax.psum_scatter(backward_terms.astype(jnp.bfloat16), 'row', scatter_dime...  91.3 us
    all_gather x1, waiting for transfers between devices, per_device(): source_block = lax.all_gather(scaled, 'row', axis=0, tiled=True)  71.1 us
    all_gather x1, waiting for transfers between devices, per_device(): upstream_block = lax.all_gather(upstream, 'col', axis=0, tiled=True)  58.1 us
    gather x6, local copies, waits for them, and re-layouts, advance(): picked = jnp.take(lookup, chosen, axis=0)  25.2 us
    dot_general x3, matrix products, advance(): jnp.einsum('tij,tif->tjf', block_tiles, picked, preferred_element_type=jn...  22.2 us
  transfers between devices with their start and end apart: 5, of which 5 were waited for; matrix products, arithmetic and copies ran while one was open for 12% of the time, Pallas kernels for 0%

commit v1 on v0

--- a/solution.py
+++ b/solution.py
@@ -79,7 +79,12 @@
     local_weight = lax.dot_general(
         aggregate, delta_rows, (((0,), (0,)), ((), ())), preferred_element_type=jnp.float32
     )
-    grad_weight = lax.psum(local_weight, ("row", "col")) / math.sqrt(total_nodes)
+
+    def _point_leaf(t0, a_name):
+        front = lax.all_gather(t0, a_name).sum(axis=0)
+        return front
+
+    grad_weight = _point_leaf(local_weight, ("row", "col")) / math.sqrt(total_nodes)
     projected = lax.dot_general(
         delta_rows, weight, (((1,), (1,)), ((), ())), preferred_element_type=jnp.float32
     )

time: 765 us -> 823 us (1.076)
  waiting for transfers between devices: 537 us -> 573 us
  other arithmetic: 113 us -> 133 us
    all_gather x0 -> x1, waiting for transfers between devices: none -> 211 us  [_point_leaf(): front = lax.all_gather(t0, a_name).sum(axis=0)]
    psum x1 -> x0, waiting for transfers between devices: 173 us -> none  [per_device(): lax.psum(local_weight, ('row', 'col')) / math.sqrt(total_nodes)]
    reduce_sum x0 -> x1, other arithmetic: none -> 21.1 us  [_point_leaf(): front = lax.all_gather(t0, a_name).sum(axis=0)]
  transfers between devices with their start and end apart: 5 -> 5, of which waited for: 5 -> 5; matrix products, arithmetic and copies ran while one was open for 12% -> 2% of each run, Pallas kernels for 0% -> 0%
where the time goes in v1:
time: 823 us; the launch traced here: 821 us
  waiting for transfers between devices  573 us (70%)
  other arithmetic  133 us (16%)
  matrix products  49.2 us (6%)
  local copies, waits for them, and re-layouts  47.3 us (6%)
  between operations  14.5 us (2%)
    all_gather x1, waiting for transfers between devices, _point_leaf(): front = lax.all_gather(t0, a_name).sum(axis=0)  211 us
    reduce_scatter x1, waiting for transfers between devices, per_device(): lax.psum_scatter(forward_terms.astype(jnp.bfloat16), 'col', scatter_dimen...  143 us
    scatter-add x6, other arithmetic, advance(): jax.ops.segment_sum(products, targets, num_segments=out_count)  96.4 us
    reduce_scatter x1, waiting for transfers between devices, per_device(): lax.psum_scatter(backward_terms.astype(jnp.bfloat16), 'row', scatter_dime...  87.7 us
    all_gather x1, waiting for transfers between devices, per_device(): source_block = lax.all_gather(scaled, 'row', axis=0, tiled=True)  71 us
    all_gather x1, waiting for transfers between devices, per_device(): upstream_block = lax.all_gather(upstream, 'col', axis=0, tiled=True)  59.9 us
    gather x6, local copies, waits for them, and re-layouts, advance(): picked = jnp.take(lookup, chosen, axis=0)  25.1 us
    dot_general x3, matrix products, advance(): jnp.einsum('tij,tif->tjf', block_tiles, picked, preferred_element_type=jn...  22.1 us
  transfers between devices with their start and end apart: 5, of which 5 were waited for; matrix products, arithmetic and copies ran while one was open for 2% of the time, Pallas kernels for 0%

profile of v1, /device:TPU:2, one launch (start us, length us, event | category | flops | bytes accessed | tf_op | source)
XLA Modules:
  0.0 820.9 jit_solution(7401669873284857490)
XLA Ops:
  12.3 71.0 %all-gather.5.cloned.1.call-done = bf16[3072,256]{1,0:T(8,128)(2,1)} async-done(((bf16[384,256]{1,0:T(8,128)(2,1)}), bf16[3072,256]{1,0:T(8,128)(2,1)}) %all-gather.5.cloned.1.call-update) | async-done | bytes 1572880 | tf_op jit(solution)/shard_map/all_gather | solution.py:57
  83.4 6.1 broadcast.23
  89.5 94.0 %while.20 = (s32[]{:T(128)}, f32[96,128,256]{2,1,0:T(8,128)}, s32[3]{0:T(128)S(1)}, s32[192]{0:T(256)S(1)}, bf16[192,128,128]{2,1,0:T(8,128)(2,1)}, /*index=5*/s...) while((s32[]{:T(128)}, f32[96,128,256]{2,1,0:T(8,128)}, ...), condition=%wide.region_2.3_spmd, body=%wide.region_0.2_spmd.sunk | while | flops 543163776 | bytes 48241480 | solution.py:35
  93.7 7.4 broadcast_multiply_fusion.5
  101.1 19.7 %scatter_fusion = f32[96,128,256]{2,1,0:T(8,128)} fusion(f32[96,128,256]{2,1,0:T(8,128)} %get-tuple-element.258, s32[64]{0:T(128)S(1)} %dynamic_slice.49, f32[64,128,256]{2,1,0:T(8,128)} %broadcast_multiply_fusion.5), kind=kCustom, calls=%fused_computation.2.clone.1 | custom fusion | flops 2097152 | bytes 25166080 | tf_op jit(solution)/shard_map/while/body/eval_jaxpr/scatter-add | solution.py:31
  125.1 7.4 broadcast_multiply_fusion.5
  132.4 19.8 %scatter_fusion = f32[96,128,256]{2,1,0:T(8,128)} fusion(f32[96,128,256]{2,1,0:T(8,128)} %get-tuple-element.258, s32[64]{0:T(128)S(1)} %dynamic_slice.49, f32[64,128,256]{2,1,0:T(8,128)} %broadcast_multiply_fusion.5), kind=kCustom, calls=%fused_computation.2.clone.1 | custom fusion | flops 2097152 | bytes 25166080 | tf_op jit(solution)/shard_map/while/body/eval_jaxpr/scatter-add | solution.py:31
  156.5 7.4 broadcast_multiply_fusion.5
  163.9 19.6 %scatter_fusion = f32[96,128,256]{2,1,0:T(8,128)} fusion(f32[96,128,256]{2,1,0:T(8,128)} %get-tuple-element.258, s32[64]{0:T(128)S(1)} %dynamic_slice.49, f32[64,128,256]{2,1,0:T(8,128)} %broadcast_multiply_fusion.5), kind=kCustom, calls=%fused_computation.2.clone.1 | custom fusion | flops 2097152 | bytes 25166080 | tf_op jit(solution)/shard_map/while/body/eval_jaxpr/scatter-add | solution.py:31
  183.4 8.1 convert_element_type.55
  192.3 143.1 %reduce-scatter.3.cloned.1.call-done = bf16[384,256]{1,0:T(8,128)(2,1)} async-done(((bf16[12288,256]{1,0:T(8,128)(2,1)}), bf16[384,256]{1,0:T(8,128)(2,1)}) %reduce-scatter.3.cloned.1.call-update) | async-done | bytes 196624 | tf_op jit(solution)/shard_map/reduce_scatter | solution.py:68
  339.0 8.7 %copy.11 = bf16[1,1,192,128,128]{3,4,2,1,0:T(8,128)(2,1)} copy(bf16[1,1,192,128,128]{4,3,2,1,0:T(8,128)(2,1)} %bitcast.25) | data formatting | bytes 12582912 | tf_op args[5]
  347.7 59.9 %all-gather.7.cloned.1.call-done = bf16[12288,256]{1,0:T(8,128)(2,1)} async-done(((bf16[384,256]{1,0:T(8,128)(2,1)}), bf16[12288,256]{1,0:T(8,128)(2,1)}) %all-gather.7.cloned.1.call-update) | async-done | bytes 6291472 | tf_op jit(solution)/shard_map/all_gather | solution.py:92
  408.0 80.7 %while.21 = (s32[]{:T(128)}, f32[24,128,256]{2,1,0:T(8,128)S(1)}, s32[3]{0:T(128)S(1)}, s32[192]{0:T(256)S(1)}, bf16[192,128,128]{1,2,0:T(8,128)(2,1)}, /*index=...) while((s32[]{:T(128)}, f32[24,128,256]{2,1,0:T(8,128)S(1)}, ...), condition=%wide.region_6.7_spmd, body=%wide.region_4.6_spmd.sunk | while | flops 543163776 | bytes 48241480 | solution.py:35
  409.5 5.6 gather_fusion.1
  415.0 7.4 broadcast_multiply_fusion.6
  422.4 12.4 %scatter_fusion.1 = f32[24,128,256]{2,1,0:T(8,128)S(1)} fusion(f32[24,128,256]{2,1,0:T(8,128)S(1)} %get-tuple-element.294, s32[64]{0:T(128)S(1)} %dynamic_slice.53, f32[64,128,256]{2,1,0:T(8,128)} %broadcast_multiply_fusion.6), kind=kCustom, calls=%fused_computation.3.clone.1 | custom fusion | flops 2097152 | bytes 25166080 | tf_op jit(solution)/shard_map/while/body/eval_jaxpr/scatter-add | solution.py:31
  441.9 7.4 broadcast_multiply_fusion.6
  449.3 12.4 %scatter_fusion.1 = f32[24,128,256]{2,1,0:T(8,128)S(1)} fusion(f32[24,128,256]{2,1,0:T(8,128)S(1)} %get-tuple-element.294, s32[64]{0:T(128)S(1)} %dynamic_slice.53, f32[64,128,256]{2,1,0:T(8,128)} %broadcast_multiply_fusion.6), kind=kCustom, calls=%fused_computation.3.clone.1 | custom fusion | flops 2097152 | bytes 25166080 | tf_op jit(solution)/shard_map/while/body/eval_jaxpr/scatter-add | solution.py:31
  468.8 7.4 broadcast_multiply_fusion.6
  476.2 12.4 %scatter_fusion.1 = f32[24,128,256]{2,1,0:T(8,128)S(1)} fusion(f32[24,128,256]{2,1,0:T(8,128)S(1)} %get-tuple-element.294, s32[64]{0:T(128)S(1)} %dynamic_slice.53, f32[64,128,256]{2,1,0:T(8,128)} %broadcast_multiply_fusion.6), kind=kCustom, calls=%fused_computation.3.clone.1 | custom fusion | flops 2097152 | bytes 25166080 | tf_op jit(solution)/shard_map/while/body/eval_jaxpr/scatter-add | solution.py:31
  492.3 87.7 %reduce-scatter.5.cloned.1.call-done = bf16[384,256]{1,0:T(8,128)(2,1)} async-done(((bf16[3072,256]{1,0:T(8,128)(2,1)}), bf16[384,256]{1,0:T(8,128)(2,1)}) %reduce-scatter.5.cloned.1.call-update) | async-done | bytes 196624 | tf_op jit(solution)/shard_map/reduce_scatter | solution.py:103
  581.9 210.7 %all-gather.9.cloned.1.call-done = f32[65536,256]{1,0:T(8,128)} async-done(((f32[256,256]{1,0:T(8,128)}), f32[65536,256]{1,0:T(8,128)}) %all-gather.9.cloned.1.call-update) | async-done | bytes 67108880 | tf_op jit(solution)/shard_map/all_gather | solution.py:84
  792.6 21.1 %reduce_sum.9 = f32[256,256]{1,0:T(8,128)S(1)} reduce(f32[256,256,256]{2,1,0:T(8,128)} %bitcast.12, f32[]{:T(128)} %constant.63.clone.1), dimensions={0}, to_apply=%region_8.9 | reduce | flops 16711680 | bytes 67371008 | tf_op jit(solution)/shard_map/reduce_sum | solution.py:84
  (79 shorter events, 39.7 us)
Async XLA Ops:
  7.2 328.2 %copy-start = (bf16[256,256]{1,0:T(8,128)(2,1)S(1)}, bf16[256,256]{1,0:T(8,128)(2,1)}, u32[]{:S(2)}) copy-start(bf16[256,256]{1,0:T(8,128)(2,1)} %param.13) | copy-start | bytes 393220
  7.2 76.2 %all-gather.5.cloned.1.call-start = ((), (), s32[]{:S(2)}) async-start(), calls=%async_computation.2 | async-start | bytes 1769472 | tf_op jit(solution)/shard_map/all_gather | solution.py:57
  8.5 0.6 copy-start.5
  10.9 324.5 %reduce-scatter.3.cloned.1.call-start = ((), (), s32[]{:S(2)}) async-start(), calls=%async_computation.3 | async-start | bytes 6488064 | tf_op jit(solution)/shard_map/reduce_scatter | solution.py:68
  83.4 6.1 copy-start.2
  191.6 0.7 copy-start.8
  191.6 143.8 %copy-start.9 = (bf16[384,256]{1,0:T(8,128)(2,1)S(1)}, bf16[384,256]{1,0:T(8,128)(2,1)}, u32[]{:S(2)}) copy-start(bf16[384,256]{1,0:T(8,128)(2,1)} %param.14) | copy-start | bytes 589828
  191.6 216.0 %all-gather.7.cloned.1.call-start = ((), (), s32[]{:S(2)}) async-start(), calls=%async_computation.4 | async-start | bytes 6488064 | tf_op jit(solution)/shard_map/all_gather | solution.py:92
  337.4 0.7 copy-start.4
  339.0 241.0 %reduce-scatter.5.cloned.1.call-start = ((), (), s32[]{:S(2)}) async-start(), calls=%async_computation.5 | async-start | bytes 1769472 | tf_op jit(solution)/shard_map/reduce_scatter | solution.py:103
  488.7 91.3 %copy-start.3 = (bf16[384,256]{1,0:T(8,128)(2,1)S(1)}, bf16[384,256]{1,0:T(8,128)(2,1)}, u32[]{:S(2)}) copy-start(bf16[384,256]{1,0:T(8,128)(2,1)} %param.12) | copy-start | bytes 589828
  488.7 91.3 %copy-start.6 = (f32[384]{0:T(512)S(1)}, f32[384]{0:T(512)}, u32[]{:S(2)}) copy-start(f32[384]{0:T(512)} %copy-done.5) | copy-start | bytes 4612
  488.7 91.3 %copy-start.7 = (f32[384]{0:T(512)S(1)}, f32[384]{0:T(512)}, u32[]{:S(2)}) copy-start(f32[384]{0:T(512)} %get-tuple-element.135) | copy-start | bytes 4612
  490.2 302.4 %all-gather.9.cloned.1.call-start = ((), (), s32[]{:S(2)}) async-start(), calls=%async_computation.6 | async-start | bytes 67371008 | tf_op jit(solution)/shard_map/all_gather | solution.py:84
  792.6 21.8 %copy-start.1 = (bf16[256,256]{1,0:T(8,128)(2,1)S(1)}, bf16[256,256]{1,0:T(8,128)(2,1)}, u32[]{:S(2)}) copy-start(bf16[256,256]{1,0:T(8,128)(2,1)} %param.13) | copy-start | bytes 393220
Sparse Core Ops, SparseCore 0:
  11.2 72.1 all-gather.4
  191.7 143.5 reduce-scatter.2
  339.1 68.4 all-gather.6
  490.3 89.6 reduce-scatter.4
  584.0 208.4 all-gather.8
